TPU v7x, 32 devices: a whole 2x2x4 slice. The times are simulated.
32 devices in a mesh: ia: 4 (over z), ja: 2 (over y), ka: 4 (over x, core).
Axes of the slice: x: 2, y: 2, z: 4, core: 2. Of those that a mesh axis runs over, the one named last changes fastest.
Arguments:
- tile_values: bfloat16 [768, 128], P(('ia', 'ja', 'ka')), may hold values from -0.59765625 to 0.59765625
- tile_rows: int32 [768, 128], P(('ia', 'ja', 'ka')), may hold values from 0 to 63
- tile_cols: int32 [768, 128], P(('ia', 'ja', 'ka')), may hold values from 0 to 2047
- tile_depths: int32 [768, 128], P(('ia', 'ja', 'ka')), may hold values from 0 to 1023
- tile_live: int32 [32, 8], P(('ia', 'ja', 'ka')), may hold values from 0 to 3, as said below
- factor_b: bfloat16 [16, 2, 2048], P(None, 'ja', ('ia', 'ka')), may hold values from -6 to 6
- factor_c: bfloat16 [16, 4, 1024], P(None, 'ka', ('ia', 'ja')), may hold values from -6 to 6
- proj: float32 [16, 256], replicated, may hold values from -0.375 to 0.375
Outputs:
- tucker_y: float32 [2048, 256], P(('ia', 'ja', 'ka'))
- gram: float32 [256, 256], replicated
- new_factor: float32 [16, 2048], P(None, ('ia', 'ja', 'ka'))
Inputs may be any that keep to these rules, and one draw needn't show every extreme that they name: tile_live[d, o] counts the live leading slots among the 3 slots that device d holds for the device at index o along ja+ka within its mode-1 block; in every draw there is an owner for which every device has all 3 slots live, and every device has some owner with all 3 slots live.
All inputs are finite; a program needn't handle non-finite values.
Results may differ from a plain program's by a relative error of at most 0.0041.
Values may be sent and summed in bfloat16 or wider, within the bound.
A program may use at most 64 MiB of HBM per device.

v0:
```python
import jax
import jax.numpy as jnp
from jax import lax
from jax.sharding import PartitionSpec as P

RANK = 16
ROWS_DEV = 64


def owner_block(scaled, depth_rows, target):
    kron_rows = (scaled[:, None] * depth_rows[None, :]).reshape(
        scaled.shape[0] * depth_rows.shape[0], -1
    )
    onehot = (target.reshape(1, -1) == lax.iota(jnp.int32, ROWS_DEV)[:, None]).astype(jnp.bfloat16)
    return lax.dot_general(
        onehot, kron_rows, (((1,), (1,)), ((), ())), preferred_element_type=jnp.float32
    )


def group_blocks(scaled, depth_rows, target, begin_slot, pair_size, slot_count):
    rank_size = scaled.shape[0]
    tile_width = scaled.shape[2]
    scaled_part = lax.dynamic_slice_in_dim(scaled, begin_slot, pair_size * slot_count, 1)
    depth_part = lax.dynamic_slice_in_dim(depth_rows, begin_slot, pair_size * slot_count, 1)
    target_part = lax.dynamic_slice_in_dim(target, begin_slot, pair_size * slot_count, 0)
    scaled_part = scaled_part.reshape(rank_size, pair_size, slot_count, tile_width)
    depth_part = depth_part.reshape(depth_rows.shape[0], pair_size, slot_count, tile_width)
    target_part = target_part.reshape(pair_size, slot_count, tile_width)
    return jax.vmap(owner_block, in_axes=(1, 1, 0))(scaled_part, depth_part, target_part)


def owner_total(scaled, depth_rows, target, groups, slot_count):
    pair_size = 2
    columns = scaled.shape[0] * depth_rows.shape[0]
    result = jnp.zeros((ROWS_DEV, columns), jnp.float32)

    def turn(turn_index, result):
        begin_slot = turn_index * pair_size * slot_count
        blocks = group_blocks(scaled, depth_rows, target, begin_slot, pair_size, slot_count)
        return result + jnp.sum(blocks, axis=0)

    return lax.fori_loop(0, groups // pair_size, turn, result)


def on_device(tile_values, tile_rows, tile_cols, tile_depths, tile_live, factor_b, factor_c, proj):
    owners = lax.axis_size("ja") * lax.axis_size("ka")
    slot_total = tile_values.shape[0]
    slot_count = slot_total // owners
    mode_two = lax.all_gather(factor_b, ("ia", "ka"), axis=2, tiled=True)[:, 0, :]
    mode_three = lax.all_gather(factor_c, ("ia", "ja"), axis=2, tiled=True)[:, 0, :]
    slot_index = lax.iota(jnp.int32, slot_total)
    owner_of = slot_index // slot_count
    counts = jnp.sum(
        jnp.where(owner_of[:, None] == lax.iota(jnp.int32, owners)[None, :], tile_live, 0), axis=1
    )
    is_live = slot_index % slot_count < counts
    target = jnp.where(is_live[:, None], tile_rows, ROWS_DEV)
    scaled = (
        tile_values.astype(jnp.float32)[None]
        * jnp.take(mode_two, tile_cols, axis=1).astype(jnp.float32)
    ).astype(jnp.bfloat16)
    depth_rows = jnp.take(mode_three, tile_depths, axis=1)
    payload = jnp.concatenate([scaled, depth_rows], axis=0)
    arrived, routed = (
        lax.all_to_all(payload, ("ja", "ka"), split_axis=1, concat_axis=1, tiled=True),
        lax.all_to_all(target[None], ("ja", "ka"), split_axis=1, concat_axis=1, tiled=True),
    )
    summed = owner_total(arrived[:RANK], arrived[RANK:], routed[0], owners, slot_count)
    local_gram = lax.dot_general(
        summed,
        summed,
        (((0,), (0,)), ((), ())),
        precision=lax.Precision.HIGHEST,
        preferred_element_type=jnp.float32,
    )
    gram_total = lax.psum(local_gram, ("ia", "ja", "ka"))
    gram = gram_total / (ROWS_DEV * owners * lax.axis_size("ia"))
    new_factor = lax.dot_general(
        proj,
        summed,
        (((1,), (1,)), ((), ())),
        precision=lax.Precision.HIGHEST,
        preferred_element_type=jnp.float32,
    )
    return (summed, gram, new_factor)


def solution(mesh):
    return jax.shard_map(
        on_device,
        mesh=mesh,
        in_specs=(
            P(("ia", "ja", "ka"), None),
            P(("ia", "ja", "ka"), None),
            P(("ia", "ja", "ka"), None),
            P(("ia", "ja", "ka"), None),
            P(("ia", "ja", "ka"), None),
            P(None, "ja", ("ia", "ka")),
            P(None, "ka", ("ia", "ja")),
            P(),
        ),
        out_specs=(P(("ia", "ja", "ka"), None), P(), P(None, ("ia", "ja", "ka"))),
        check_vma=False,
    )
```

profile of v0, /device:TPU:0, one launch (start us, length us, event | category | flops | bytes accessed | tf_op | source)
XLA Modules:
  0.0 239.9 jit_solution(6678735856828618585)
XLA Ops:
  7.2 0.8 bitcast_clamp_fusion.1
  8.0 0.7 copy-done.3
  8.7 0.7 copy-done.6
  9.5 24.6 %all_gather.6 = bf16[16,1,2048]{0,2,1:T(8,128)(2,1)S(1)} all-gather(bf16[16,1,128]{0,2,1:T(8,128)(2,1)S(1)} %copy.29), channel_id=1, replica_groups=mesh['ia'=4,'ja'=2,'ka'=4] {'ia','ka'}, dimensions={2}, use_global_device_ids=true | all-gather | bytes 69632 | tf_op jit(solution)/shard_map/all_gather | solution.py:49
  34.1 9.2 %gather_fusion = bf16[3072,16]{1,0:T(8,128)(2,1)S(1)} fusion(bf16[16,2048]{0,1:T(8,128)(2,1)S(1)} %bitcast.41, s32[3072]{0:T(1024)S(1)} %bitcast_clamp_fusion.1), kind=kCustom, calls=%fused_computation | custom fusion | bytes 208896 | tf_op jit(solution)/shard_map/jit(_take)/gather | solution.py:60
  43.3 0.3 copy.30
  43.5 0.4 copy-done.5
  44.0 0.7 copy-done.7
  44.8 30.8 %all_gather.7 = bf16[16,1,1024]{0,2,1:T(8,128)(2,1)S(1)} all-gather(bf16[16,1,128]{0,2,1:T(8,128)(2,1)S(1)} %copy.31), channel_id=1, replica_groups=mesh['ia'=4,'ja'=2,'ka'=4] {'ia','ja'}, dimensions={2}, use_global_device_ids=true | all-gather | bytes 36864 | tf_op jit(solution)/shard_map/all_gather | solution.py:50
  75.5 9.2 %gather_fusion.1 = bf16[3072,16]{1,0:T(8,128)(2,1)S(1)} fusion(bf16[16,1024]{0,1:T(8,128)(2,1)S(1)} %bitcast.40, s32[3072]{0:T(1024)S(1)} %bitcast_clamp_fusion), kind=kCustom, calls=%fused_computation.1 | custom fusion | bytes 208896 | tf_op jit(solution)/shard_map/jit(_take)/gather | solution.py:62
  84.7 0.3 copy.32
  85.0 0.7 pad_maximum_fusion
  85.7 3.5 %all-to-all-start.1 = ((bf16[32,24,128]{2,0,1:T(8,128)(2,1)}), bf16[32,24,128]{2,0,1:T(8,128)(2,1)S(1)}, u32[]{:S(2)}, u32[]{:S(2)}) async-start(bf16[32,24,128]{2,0,1:T(8,128)(2,1)} %pad_maximum_fusion), calls=%async_computation.1 | async-start | bytes 393216 | tf_op jit(solution)/shard_map/all_to_all | solution.py:65
  89.3 0.6 copy-done.8
  90.1 0.7 broadcast_select_fusion
  90.7 4.7 %all-to-all-done.1 = bf16[32,24,128]{2,0,1:T(8,128)(2,1)S(1)} async-done(((bf16[32,24,128]{2,0,1:T(8,128)(2,1)}), bf16[32,24,128]{2,0,1:T(8,128)(2,1)S(1)}, u32[]{:S(2)}, u32[]{:S(2)}) %all-to-all-start.1) | async-done | bytes 196640 | tf_op jit(solution)/shard_map/all_to_all | solution.py:65
  95.4 3.3 %all-to-all-start = ((s32[1,24,128]{2,0,1:T(1,128)}), s32[1,24,128]{2,0,1:T(1,128)S(1)}, u32[]{:S(2)}, u32[]{:S(2)}) async-start(s32[1,24,128]{2,0,1:T(1,128)} %bitcast.1), calls=%async_computation | async-start | bytes 24576 | tf_op jit(solution)/shard_map/all_to_all | solution.py:66
  98.8 4.6 %all-to-all-done = s32[1,24,128]{2,0,1:T(1,128)S(1)} async-done(((s32[1,24,128]{2,0,1:T(1,128)}), s32[1,24,128]{2,0,1:T(1,128)S(1)}, u32[]{:S(2)}, u32[]{:S(2)}) %all-to-all-start) | async-done | bytes 12320 | tf_op jit(solution)/shard_map/all_to_all | solution.py:66
  103.4 3.7 %while.16 = (s32[]{:T(128)}, f32[64,256]{1,0:T(8,128)S(1)}, s32[24,128]{1,0:T(8,128)S(1)}, bf16[16,24,128]{2,0,1:T(8,128)(2,1)S(1)}, bf16[16,24,128]{2,0,1:T(8,1...) while((s32[]{:T(128)}, f32[64,256]{1,0:T(8,128)S(1)}, s32[24,128]{1,0:T(8,128)S(1)}, ...), condition=%wide.region_2.3_spmd.clone, body=%wide.region_1.2_spmd.clone.sunk | while | flops 25444360 | bytes 1965213 | solution.py:42
  103.7 0.3 mul.80
  104.0 0.3 fusion.14
  104.4 0.2 broadcast_multiply_fusion.3
  104.6 0.3 mul.80
  105.0 0.3 fusion.14
  105.5 0.3 mul.80
  105.9 0.3 fusion.14
  106.5 0.3 mul.80
  106.9 0.3 fusion.14
  107.2 1.1 fusion.5
  108.3 0.8 convolution_bitcast_fusion.1
  109.1 122.3 %all-reduce.2.cloned.1.call-done = f32[256,256]{1,0:T(8,128)} async-done(((f32[256,256]{1,0:T(8,128)}), f32[256,256]{1,0:T(8,128)}) %all-reduce.2.cloned.1.call-update) | async-done | bytes 262160 | tf_op jit(solution)/shard_map/psum | solution.py:76
  231.4 1.7 broadcast_multiply_fusion.1
  (51 shorter events, 1.4 us)
Async XLA Ops:
  7.2 101.2 %copy-start = (f32[16,256]{1,0:T(8,128)S(1)}, f32[16,256]{1,0:T(8,128)}, u32[]{:S(2)}) copy-start(f32[16,256]{1,0:T(8,128)} %param.17) | copy-start | bytes 49156
  7.2 0.8 copy-start.2
  8.0 0.7 copy-start.3
  8.7 0.7 copy-start.6
  43.3 0.7 copy-start.5
  44.0 0.7 copy-start.7
  85.7 4.3 %copy-start.4 = (s32[24,128]{1,0:T(8,128)S(1)}, s32[24,128]{1,0:T(8,128)}, u32[]{:S(2)}) copy-start(s32[24,128]{1,0:T(8,128)} %param.11) | copy-start | bytes 36868
  85.7 9.7 %all-to-all-start.1 = ((bf16[32,24,128]{2,0,1:T(8,128)(2,1)}), bf16[32,24,128]{2,0,1:T(8,128)(2,1)S(1)}, u32[]{:S(2)}, u32[]{:S(2)}) async-start(bf16[32,24,128]{2,0,1:T(8,128)(2,1)} %pad_maximum_fusion), calls=%async_computation.1 | async-start | bytes 393216 | tf_op jit(solution)/shard_map/all_to_all | solution.py:65
  89.3 0.7 copy-start.8
  95.4 8.0 %all-to-all-start = ((s32[1,24,128]{2,0,1:T(1,128)}), s32[1,24,128]{2,0,1:T(1,128)S(1)}, u32[]{:S(2)}, u32[]{:S(2)}) async-start(s32[1,24,128]{2,0,1:T(1,128)} %bitcast.1), calls=%async_computation | async-start | bytes 24576 | tf_op jit(solution)/shard_map/all_to_all | solution.py:66
  98.7 132.6 %all-reduce.2.cloned.1.call-start = ((), (), s32[]{:S(2)}) async-start(), calls=%async_computation.2 | async-start | bytes 524288 | tf_op jit(solution)/shard_map/psum | solution.py:76
  107.1 1.2 copy-start.1
Sparse Core Ops, SparseCore 0:
  108.4 122.8 all-reduce.1
where the time goes:
time: 240 us
  waiting for transfers between devices  132 us (55%)
  blocking collectives  55.4 us (23%)
  local copies, waits for them, and re-layouts  23.8 us (10%)
  between operations  14.2 us (6%)
  starting transfers between devices  6.9 us (3%)
  other arithmetic  4.78 us (2%)
  matrix products  2.99 us (1%)
    psum x1, waiting for transfers between devices, on_device(): gram_total = lax.psum(local_gram, ('ia', 'ja', 'ka'))  122 us
    all_gather x1, blocking collectives, on_device(): lax.all_gather(factor_c, ('ia', 'ja'), axis=2, tiled=True)[:, 0, :]  30.8 us
    all_gather x1, blocking collectives, on_device(): lax.all_gather(factor_b, ('ia', 'ka'), axis=2, tiled=True)[:, 0, :]  24.6 us
    gather x2, local copies, waits for them, and re-layouts, on_device(): depth_rows = jnp.take(mode_three, tile_depths, axis=1)  9.41 us
    gather x2, local copies, waits for them, and re-layouts, on_device(): jnp.take(mode_two, tile_cols, axis=1).astype(jnp.float32)  9.41 us
  transfers between devices with their start and end apart: 3, of which 3 were waited for; matrix products, arithmetic and copies ran while one was open for 1% of the time, Pallas kernels for 0%

commit v1 on v0

--- a/solution.py
+++ b/solution.py
@@ -73,7 +73,7 @@
         precision=lax.Precision.HIGHEST,
         preferred_element_type=jnp.float32,
     )
-    gram_total = lax.psum(local_gram, ("ia", "ja", "ka"))
+    gram_total = lax.psum(lax.psum(local_gram, ("ja", "ka")), "ia")
     gram = gram_total / (ROWS_DEV * owners * lax.axis_size("ia"))
     new_factor = lax.dot_general(
         proj,

time: 240 us -> 205 us (0.85)
  waiting for transfers between devices: 132 us -> 96.2 us
    psum x1 -> x2, waiting for transfers between devices: 122 us -> 86.9 us  [on_device(): gram_total = lax.psum(lax.psum(local_gram, ('ja', 'ka')), 'ia')]
  transfers between devices with their start and end apart: 3 -> 4, of which waited for: 3 -> 4; matrix products, arithmetic and copies ran while one was open for 1% -> 1% of each run, Pallas kernels for 0% -> 0%
where the time goes in v1:
time: 205 us
  waiting for transfers between devices  96.2 us (47%)
  blocking collectives  55.4 us (27%)
  local copies, waits for them, and re-layouts  23.8 us (12%)
  between operations  14.2 us (7%)
  starting transfers between devices  6.94 us (3%)
  other arithmetic  4.78 us (2%)
  matrix products  2.99 us (1%)
    psum x2, waiting for transfers between devices, on_device(): gram_total = lax.psum(lax.psum(local_gram, ('ja', 'ka')), 'ia')  86.9 us
    all_gather x1, blocking collectives, on_device(): lax.all_gather(factor_c, ('ia', 'ja'), axis=2, tiled=True)[:, 0, :]  30.8 us
    all_gather x1, blocking collectives, on_device(): lax.all_gather(factor_b, ('ia', 'ka'), axis=2, tiled=True)[:, 0, :]  24.6 us
    gather x2, local copies, waits for them, and re-layouts, on_device(): depth_rows = jnp.take(mode_three, tile_depths, axis=1)  9.41 us
    gather x2, local copies, waits for them, and re-layouts, on_device(): jnp.take(mode_two, tile_cols, axis=1).astype(jnp.float32)  9.41 us
    all_to_all x1, waiting for transfers between devices, on_device(): lax.all_to_all(payload, ('ja', 'ka'), split_axis=1, concat_axis=1, tiled=...  4.68 us
    all_to_all x1, waiting for transfers between devices, on_device(): lax.all_to_all(target[None], ('ja', 'ka'), split_axis=1, concat_axis=1, t...  4.59 us
  transfers between devices with their start and end apart: 4, of which 4 were waited for; matrix products, arithmetic and copies ran while one was open for 1% of the time, Pallas kernels for 0%

profile of v1, /device:TPU:0, one launch (start us, length us, event | category | flops | bytes accessed | tf_op | source)
XLA Modules:
  0.0 204.5 jit_solution(6119360781119444534)
XLA Ops:
  7.2 0.8 bitcast_clamp_fusion.1
  8.0 0.7 copy-done.3
  8.7 0.7 copy-done.6
  9.5 24.6 %all_gather.6 = bf16[16,1,2048]{0,2,1:T(8,128)(2,1)S(1)} all-gather(bf16[16,1,128]{0,2,1:T(8,128)(2,1)S(1)} %copy.29), channel_id=1, replica_groups=mesh['ia'=4,'ja'=2,'ka'=4] {'ia','ka'}, dimensions={2}, use_global_device_ids=true | all-gather | bytes 69632 | tf_op jit(solution)/shard_map/all_gather | solution.py:49
  34.1 9.2 %gather_fusion = bf16[3072,16]{1,0:T(8,128)(2,1)S(1)} fusion(bf16[16,2048]{0,1:T(8,128)(2,1)S(1)} %bitcast.41, s32[3072]{0:T(1024)S(1)} %bitcast_clamp_fusion.1), kind=kCustom, calls=%fused_computation | custom fusion | bytes 208896 | tf_op jit(solution)/shard_map/jit(_take)/gather | solution.py:60
  43.3 0.3 copy.30
  43.5 0.4 copy-done.5
  44.0 0.7 copy-done.7
  44.8 30.8 %all_gather.7 = bf16[16,1,1024]{0,2,1:T(8,128)(2,1)S(1)} all-gather(bf16[16,1,128]{0,2,1:T(8,128)(2,1)S(1)} %copy.31), channel_id=1, replica_groups=mesh['ia'=4,'ja'=2,'ka'=4] {'ia','ja'}, dimensions={2}, use_global_device_ids=true | all-gather | bytes 36864 | tf_op jit(solution)/shard_map/all_gather | solution.py:50
  75.5 9.2 %gather_fusion.1 = bf16[3072,16]{1,0:T(8,128)(2,1)S(1)} fusion(bf16[16,1024]{0,1:T(8,128)(2,1)S(1)} %bitcast.40, s32[3072]{0:T(1024)S(1)} %bitcast_clamp_fusion), kind=kCustom, calls=%fused_computation.1 | custom fusion | bytes 208896 | tf_op jit(solution)/shard_map/jit(_take)/gather | solution.py:62
  84.7 0.3 copy.32
  85.0 0.7 pad_maximum_fusion
  85.7 3.5 %all-to-all-start.1 = ((bf16[32,24,128]{2,0,1:T(8,128)(2,1)}), bf16[32,24,128]{2,0,1:T(8,128)(2,1)S(1)}, u32[]{:S(2)}, u32[]{:S(2)}) async-start(bf16[32,24,128]{2,0,1:T(8,128)(2,1)} %pad_maximum_fusion), calls=%async_computation.1 | async-start | bytes 393216 | tf_op jit(solution)/shard_map/all_to_all | solution.py:65
  89.3 0.6 copy-done.8
  90.1 0.7 broadcast_select_fusion
  90.7 4.7 %all-to-all-done.1 = bf16[32,24,128]{2,0,1:T(8,128)(2,1)S(1)} async-done(((bf16[32,24,128]{2,0,1:T(8,128)(2,1)}), bf16[32,24,128]{2,0,1:T(8,128)(2,1)S(1)}, u32[]{:S(2)}, u32[]{:S(2)}) %all-to-all-start.1) | async-done | bytes 196640 | tf_op jit(solution)/shard_map/all_to_all | solution.py:65
  95.4 3.3 %all-to-all-start = ((s32[1,24,128]{2,0,1:T(1,128)}), s32[1,24,128]{2,0,1:T(1,128)S(1)}, u32[]{:S(2)}, u32[]{:S(2)}) async-start(s32[1,24,128]{2,0,1:T(1,128)} %bitcast.1), calls=%async_computation | async-start | bytes 24576 | tf_op jit(solution)/shard_map/all_to_all | solution.py:66
  98.8 4.6 %all-to-all-done = s32[1,24,128]{2,0,1:T(1,128)S(1)} async-done(((s32[1,24,128]{2,0,1:T(1,128)}), s32[1,24,128]{2,0,1:T(1,128)S(1)}, u32[]{:S(2)}, u32[]{:S(2)}) %all-to-all-start) | async-done | bytes 12320 | tf_op jit(solution)/shard_map/all_to_all | solution.py:66
  103.4 3.7 %while.16 = (s32[]{:T(128)}, f32[64,256]{1,0:T(8,128)S(1)}, s32[24,128]{1,0:T(8,128)S(1)}, bf16[16,24,128]{2,0,1:T(8,128)(2,1)S(1)}, bf16[16,24,128]{2,0,1:T(8,1...) while((s32[]{:T(128)}, f32[64,256]{1,0:T(8,128)S(1)}, s32[24,128]{1,0:T(8,128)S(1)}, ...), condition=%wide.region_2.3_spmd.clone, body=%wide.region_1.2_spmd.clone.sunk | while | flops 25444360 | bytes 1965213 | solution.py:42
  103.7 0.3 mul.80
  104.0 0.3 fusion.14
  104.6 0.3 mul.80
  105.0 0.3 fusion.14
  105.5 0.3 mul.80
  105.9 0.3 fusion.14
  106.5 0.3 mul.80
  106.9 0.3 fusion.14
  107.2 1.1 fusion.5
  108.4 50.3 %all-reduce.3.cloned.1.call-done = f32[256,256]{1,0:T(8,128)} async-done(((f32[256,256]{1,0:T(8,128)}), f32[256,256]{1,0:T(8,128)}) %all-reduce.3.cloned.1.call-update) | async-done | bytes 262160 | tf_op jit(solution)/shard_map/psum | solution.py:76
  158.7 0.8 convolution_bitcast_fusion.1
  159.5 36.5 %all-reduce.5.cloned.1.call-done = f32[256,256]{1,0:T(8,128)} async-done(((f32[256,256]{1,0:T(8,128)}), f32[256,256]{1,0:T(8,128)}) %all-reduce.5.cloned.1.call-update) | async-done | bytes 262160 | tf_op jit(solution)/shard_map/psum | solution.py:76
  196.0 1.7 broadcast_multiply_fusion.1
  (54 shorter events, 1.6 us)
Async XLA Ops:
  7.2 151.6 %copy-start = (f32[16,256]{1,0:T(8,128)S(1)}, f32[16,256]{1,0:T(8,128)}, u32[]{:S(2)}) copy-start(f32[16,256]{1,0:T(8,128)} %param.17) | copy-start | bytes 49156
  7.2 0.8 copy-start.2
  8.0 0.7 copy-start.3
  8.7 0.7 copy-start.6
  43.3 0.7 copy-start.5
  44.0 0.7 copy-start.7
  85.7 4.3 %copy-start.4 = (s32[24,128]{1,0:T(8,128)S(1)}, s32[24,128]{1,0:T(8,128)}, u32[]{:S(2)}) copy-start(s32[24,128]{1,0:T(8,128)} %param.11) | copy-start | bytes 36868
  85.7 9.7 %all-to-all-start.1 = ((bf16[32,24,128]{2,0,1:T(8,128)(2,1)}), bf16[32,24,128]{2,0,1:T(8,128)(2,1)S(1)}, u32[]{:S(2)}, u32[]{:S(2)}) async-start(bf16[32,24,128]{2,0,1:T(8,128)(2,1)} %pad_maximum_fusion), calls=%async_computation.1 | async-start | bytes 393216 | tf_op jit(solution)/shard_map/all_to_all | solution.py:65
  89.3 0.7 copy-start.8
  95.4 8.0 %all-to-all-start = ((s32[1,24,128]{2,0,1:T(1,128)}), s32[1,24,128]{2,0,1:T(1,128)S(1)}, u32[]{:S(2)}, u32[]{:S(2)}) async-start(s32[1,24,128]{2,0,1:T(1,128)} %bitcast.1), calls=%async_computation | async-start | bytes 24576 | tf_op jit(solution)/shard_map/all_to_all | solution.py:66
  98.7 59.9 %all-reduce.3.cloned.1.call-start = ((), (), s32[]{:S(2)}) async-start(), calls=%async_computation.2 | async-start | bytes 524288 | tf_op jit(solution)/shard_map/psum | solution.py:76
  107.1 51.6 %copy-start.1 = (f32[64,256]{1,0:T(8,128)}, f32[64,256]{1,0:T(8,128)S(1)}, u32[]{:S(2)}) copy-start(f32[64,256]{1,0:T(8,128)S(1)} %get-tuple-element.132) | copy-start | bytes 196612
  108.3 87.7 %all-reduce.5.cloned.1.call-start = ((), (), s32[]{:S(2)}) async-start(), calls=%async_computation.3 | async-start | bytes 524288 | tf_op jit(solution)/shard_map/psum | solution.py:76
Sparse Core Ops, SparseCore 0:
  108.4 50.2 all-reduce.2
  161.0 34.9 all-reduce.4
